TPU v7x, 512 devices: a whole 4x4x16 slice. The times are simulated.
512 devices in a mesh: tok: 16 (over z_hi, y), feat: 32 (over x, z_lo, core).
Axes of the slice: x: 4, y: 4, z: 16 (z_hi: 4, z_lo: 4; z = z_hi * 4 + z_lo), core: 2. Of those that a mesh axis runs over, the one named last changes fastest.
Arguments:
- tokens: bfloat16 [1024, 8192], P('tok', 'feat'), may hold values from -6 to 6
- gain: float32 [8192], replicated, may hold values from 0.1 to 1.9
- proj: bfloat16 [8192, 8192], P('tok', 'feat'), may hold values from -0.0625 to 0.0625
- panel_index: int32 [1], replicated, may hold values from 0 to 31
Outputs:
- panel_rows: float32 [256, 8192], P(None, 'feat')
- solved_cross: float32 [256, 8192], P(None, 'feat')
All inputs are finite; a program needn't handle non-finite values.
Results may differ from a plain program's by a relative error of at most 0.01.
Values may be sent and summed in bfloat16 or wider, within the bound.
No kernel may reach another device: no remote copies, remote signals or barrier semaphores. Data moves between devices by JAX's collectives and lax.ppermute only.
A program may use at most 64 MiB of HBM per device.

v0:
```python
import math
import jax
import jax.numpy as jnp
from jax import lax
from jax.sharding import PartitionSpec as P

D = 8192
PANEL = 256


def solve_pair(factor, gram_part, cross_part):
    first = lax.linalg.triangular_solve(factor, gram_part, left_side=True, lower=True)
    second = lax.linalg.triangular_solve(factor, cross_part, left_side=True, lower=True)
    return (first, second)


def body(tokens, gain, proj, panel_index):
    token_full = lax.all_gather(tokens, "feat", axis=1, tiled=True)
    wide_rows = token_full.astype(jnp.float32)
    inv_rms = lax.rsqrt(jnp.mean(wide_rows * wide_rows, axis=1, keepdims=True) + 1e-05)
    normed = (wide_rows * inv_rms * gain[None, :]).astype(jnp.bfloat16)
    local_cols = tokens.shape[1]
    projected = jnp.dot(
        normed, lax.all_gather(proj, "tok", axis=0, tiled=True), preferred_element_type=jnp.float32
    )
    own_values = tokens.astype(jnp.float32)
    outputs = (own_values + projected).astype(jnp.bfloat16)
    change = (outputs.astype(jnp.float32) - own_values).astype(jnp.bfloat16)
    band_start = panel_index[0] * PANEL
    band_cols = lax.dynamic_slice_in_dim(token_full, band_start, PANEL, 1)
    gram_part = jnp.dot(band_cols.T, tokens, preferred_element_type=jnp.float32)
    cross_part = jnp.dot(band_cols.T, change, preferred_element_type=jnp.float32)
    gram_sum, cross_sum = (
        lax.psum_scatter(gram_part, "tok", scatter_dimension=0, tiled=True),
        lax.psum_scatter(cross_part, "tok", scatter_dimension=0, tiled=True),
    )
    tok_count = lax.axis_size("tok")
    feat_count = lax.axis_size("feat")
    token_count = tokens.shape[0] * tok_count
    rows_here = gram_sum.shape[0]
    row_ids = lax.broadcasted_iota(jnp.int32, gram_sum.shape, 0) + lax.axis_index("tok") * rows_here
    col_ids = (
        lax.broadcasted_iota(jnp.int32, gram_sum.shape, 1) + lax.axis_index("feat") * local_cols
    )
    ridge_mask = jnp.where(col_ids == row_ids + band_start, 0.1, 0.0).astype(jnp.float32)
    gram_rows = gram_sum / token_count + ridge_mask
    cross_rows = cross_sum * (math.sqrt(D) / token_count)
    slab_rows = PANEL // feat_count
    own_slab = lax.dynamic_slice_in_dim(band_cols, lax.axis_index("feat") * slab_rows, slab_rows, 1)
    partial_value = jnp.dot(own_slab.T, band_cols, preferred_element_type=jnp.float32)
    summed = lax.psum(partial_value, "tok")
    diag_sum = lax.all_gather(summed, "feat", axis=0, tiled=True)
    diag_block = diag_sum / token_count + 0.1 * jnp.eye(PANEL, dtype=jnp.float32)
    factor = jnp.linalg.cholesky(diag_block)
    gram_all, cross_all = (
        lax.all_gather(gram_rows, "tok", axis=0, tiled=True),
        lax.all_gather(cross_rows, "tok", axis=0, tiled=True),
    )
    panel_rows, solved_cross = solve_pair(factor, gram_all, cross_all)
    return (panel_rows, solved_cross)


def solution(mesh):
    return jax.shard_map(
        body,
        mesh=mesh,
        in_specs=(P("tok", "feat"), P(), P("tok", "feat"), P()),
        out_specs=(P(None, "feat"), P(None, "feat")),
        check_vma=False,
    )
```

profile of v0, /device:TPU:6, one launch (start us, length us, event | category | flops | bytes accessed | tf_op | source)
XLA Modules:
  0.0 510.4 jit_solution(6681423414111467340)
XLA Ops:
  7.2 0.0 all-gather.3.cloned.1.call-start
  7.2 0.7 all-gather.3.cloned.1.call-update
  7.9 0.0 reduce-scatter.3.cloned.1.call-start
  8.6 70.5 %all-gather.3.cloned.1.call-done = bf16[64,8192]{1,0:T(8,128)(2,1)} async-done(((bf16[64,256]{1,0:T(8,128)(2,1)}), bf16[64,8192]{1,0:T(8,128)(2,1)}) %all-gather.3.cloned.1.call-update) | async-done | bytes 1048592 | tf_op jit(solution)/shard_map/all_gather | solution.py:18
  79.0 1.7 fusion.28
  80.7 0.0 reduce-scatter.3.cloned.1.call-update
  80.8 0.0 all-gather.5.cloned.1.call-start
  80.8 0.7 all-gather.5.cloned.1.call-update
  81.5 0.0 reduce-scatter.5.cloned.1.call-start
  81.6 1.1 fusion.30
  82.7 53.7 %psum.7 = f32[8,256]{1,0:T(8,128)S(1)} all-reduce(f32[8,256]{1,0:T(8,128)S(1)} %fusion.30), channel_id=1, replica_groups=mesh['tok'=16,'feat'=32] {'tok'}, use_global_device_ids=true, to_apply=%region_0.0 | all-reduce | flops 2048 | bytes 16384 | tf_op jit(solution)/shard_map/psum | solution.py:51
  136.4 36.4 %all_gather.16 = f32[256,256]{1,0:T(8,128)S(1)} all-gather(f32[8,256]{1,0:T(8,128)S(1)} %psum.7), channel_id=1, replica_groups=mesh['tok'=16,'feat'=32] {'feat'}, dimensions={0}, use_global_device_ids=true | all-gather | bytes 270336 | tf_op jit(solution)/shard_map/all_gather | solution.py:52
  172.8 0.1 copy.13
  173.0 0.1 copy.14
  173.1 0.1 fusion.14
  173.2 11.7 %cholesky.49 = f32[128,128]{1,0:T(8,128)S(1)} custom-call(f32[128,128]{1,0:T(8,128)S(1)} %cholesky.115), custom_call_target="Cholesky" | custom-call | tf_op jit(solution)/shard_map/jit(cholesky)/cholesky | solution.py:54
  184.9 0.1 copy.15
  185.0 0.0 copy-start
  185.0 9.8 %custom-call.14 = f32[1,128,128]{1,2,0:T(8,128)S(1)} custom-call(f32[1,128,128]{2,1,0:T(8,128)S(1)} %get-tuple-element.46), custom_call_target="InvertDiagBlocksLowerTriangular" | custom-call | tf_op jit(solution)/shard_map/jit(cholesky)/cholesky | solution.py:54
  194.8 0.2 fusion.19
  195.1 0.1 copy.16
  195.2 0.3 convolution_subtract_fusion.2
  195.4 11.7 %cholesky.103 = f32[128,128]{1,0:T(8,128)S(1)} custom-call(f32[128,128]{1,0:T(8,128)S(1)} %convolution_subtract_fusion.2), custom_call_target="Cholesky" | custom-call | tf_op jit(solution)/shard_map/jit(cholesky)/cholesky | solution.py:54
  207.1 0.1 copy.17
  207.3 0.7 compare_reduce_fusion
  209.4 0.0 copy-start.1
  209.4 0.0 copy-start.2
  209.5 0.1 broadcast.136
  209.5 4.5 while.4
  209.7 0.6 fusion.46
  210.3 1.4 dynamic-slice.9
  211.7 0.1 copy.22
  211.9 0.6 fusion.46
  212.5 1.4 dynamic-slice.9
  213.9 0.1 copy.22
  214.0 19.7 %custom-call.16 = f32[2,128,128]{1,2,0:T(8,128)S(1)} custom-call(f32[2,128,128]{2,1,0:T(8,128)S(1)} %get-tuple-element.17), custom_call_target="InvertDiagBlocksLowerTriangular" | custom-call | tf_op jit(solution)/shard_map/triangular_solve/custom-call.0 | solution.py:12
  233.7 0.0 copy-done
  233.7 0.3 fusion
  234.0 0.0 reduce-scatter.3.cloned.1.call-done
  234.0 0.8 select_add_fusion.1
  234.8 67.7 %all_gather.17 = f32[256,256]{1,0:T(8,128)S(1)} all-gather(f32[16,256]{1,0:T(8,128)S(1)} %select_add_fusion.1), channel_id=1, replica_groups=mesh['tok'=16,'feat'=32] {'tok'}, dimensions={0}, use_global_device_ids=true | all-gather | bytes 278528 | tf_op jit(solution)/shard_map/all_gather | solution.py:56
  302.5 0.3 fusion.17
  302.9 24.7 %all-gather.5.cloned.1.call-done = bf16[8192,256]{1,0:T(8,128)(2,1)} async-done(((bf16[512,256]{1,0:T(8,128)(2,1)}), bf16[8192,256]{1,0:T(8,128)(2,1)}) %all-gather.5.cloned.1.call-update) | async-done | bytes 4194320 | tf_op jit(solution)/shard_map/all_gather | solution.py:24
  327.6 0.0 copy-done.1
  327.6 0.0 copy-done.2
  327.6 4.0 fusion.7
  331.6 0.0 reduce-scatter.5.cloned.1.call-update
  331.6 0.3 convolution_subtract_fusion.1
  331.9 0.3 fusion.24
  332.3 0.7 pad_maximum_fusion
  333.0 115.6 %reduce-scatter.5.cloned.1.call-done = f32[16,256]{1,0:T(8,128)} async-done(((f32[256,256]{1,0:T(8,128)}), f32[16,256]{1,0:T(8,128)}) %reduce-scatter.5.cloned.1.call-update) | async-done | bytes 16400 | tf_op jit(solution)/shard_map/reduce_scatter | solution.py:35
  448.6 0.7 broadcast_multiply_fusion
  449.3 52.8 %all_gather.19 = f32[256,256]{1,0:T(8,128)S(1)} all-gather(f32[16,256]{1,0:T(8,128)S(1)} %broadcast_multiply_fusion), channel_id=1, replica_groups=mesh['tok'=16,'feat'=32] {'tok'}, dimensions={0}, use_global_device_ids=true | all-gather | bytes 278528 | tf_op jit(solution)/shard_map/all_gather | solution.py:57
  502.2 0.3 fusion.15
  502.5 0.3 convolution_subtract_fusion
  502.8 0.3 fusion.23
  503.1 0.7 pad_maximum_fusion.1
  (17 shorter events, 0.2 us)
Async XLA Ops:
  7.2 71.9 %all-gather.3.cloned.1.call-start = ((), (), s32[]{:S(2)}) async-start(), calls=%async_computation.2 | async-start | bytes 1081344 | tf_op jit(solution)/shard_map/all_gather | solution.py:18
  7.9 226.1 %reduce-scatter.3.cloned.1.call-start = ((), (), s32[]{:S(2)}) async-start(), calls=%async_computation.3 | async-start | bytes 278528 | tf_op jit(solution)/shard_map/reduce_scatter | solution.py:34
  80.8 246.8 %all-gather.5.cloned.1.call-start = ((), (), s32[]{:S(2)}) async-start(), calls=%async_computation.4 | async-start | bytes 4456448 | tf_op jit(solution)/shard_map/all_gather | solution.py:24
  81.5 367.1 %reduce-scatter.5.cloned.1.call-start = ((), (), s32[]{:S(2)}) async-start(), calls=%async_computation.5 | async-start | bytes 278528 | tf_op jit(solution)/shard_map/reduce_scatter | solution.py:35
  185.0 48.7 %copy-start = (bf16[64,8192]{1,0:T(8,128)(2,1)S(1)}, bf16[64,8192]{1,0:T(8,128)(2,1)}, u32[]{:S(2)}) copy-start(bf16[64,8192]{1,0:T(8,128)(2,1)} %all-gather.3.cloned.1.call-done) | copy-start | bytes 3145732
  209.4 118.2 %copy-start.1 = (bf16[64,256]{1,0:T(8,128)(2,1)S(1)}, bf16[64,256]{1,0:T(8,128)(2,1)}, u32[]{:S(2)}) copy-start(bf16[64,256]{1,0:T(8,128)(2,1)} %param.6) | copy-start | bytes 98308
  209.4 118.2 %copy-start.2 = (f32[8192]{0:T(1024)S(1)}, f32[8192]{0:T(1024)}, u32[]{:S(2)}) copy-start(f32[8192]{0:T(1024)} %param.7) | copy-start | bytes 98308
Sparse Core Ops, SparseCore 0:
  10.0 68.9 all-gather.2
  83.7 113.0 reduce-scatter.2
  199.7 127.8 all-gather.4
  332.1 116.5 reduce-scatter.4
where the time goes:
time: 511 us; the launch traced here: 510 us
  waiting for transfers between devices  212 us (41%)
  blocking collectives  211 us (41%)
  other arithmetic  57.1 us (11%)
  between operations  16 us (3%)
  matrix products  9.1 us (2%)
    reduce_scatter x1, waiting for transfers between devices, body(): lax.psum_scatter(cross_part, 'tok', scatter_dimension=0, tiled=True)  116 us
    all_gather x1, waiting for transfers between devices, body(): token_full = lax.all_gather(tokens, 'feat', axis=1, tiled=True)  70.5 us
    all_gather x1, blocking collectives, body(): lax.all_gather(gram_rows, 'tok', axis=0, tiled=True)  67.7 us
    psum x1, blocking collectives, body(): summed = lax.psum(partial_value, 'tok')  53.7 us
    all_gather x1, blocking collectives, body(): lax.all_gather(cross_rows, 'tok', axis=0, tiled=True)  52.8 us
    all_gather x1, blocking collectives, body(): diag_sum = lax.all_gather(summed, 'feat', axis=0, tiled=True)  36.4 us
    another operation x6, other arithmetic, body(): factor = jnp.linalg.cholesky(diag_block)  34 us
    all_gather x1, waiting for transfers between devices, body(): lax.all_gather(proj, 'tok', axis=0, tiled=True)  24.7 us
  transfers between devices with their start and end apart: 4, of which 3 were waited for; matrix products, arithmetic and copies ran while one was open for 12% of the time, Pallas kernels for 0%

commit v1 on v0

--- a/solution.py
+++ b/solution.py
@@ -54,7 +54,9 @@
     factor = jnp.linalg.cholesky(diag_block)
     gram_all, cross_all = (
         lax.all_gather(gram_rows, "tok", axis=0, tiled=True),
-        lax.all_gather(cross_rows, "tok", axis=0, tiled=True),
+        jnp.concatenate(
+            lax.all_to_all(jnp.stack([cross_rows] * lax.axis_size("tok")), "tok", 0, 0), axis=0
+        ),
     )
     panel_rows, solved_cross = solve_pair(factor, gram_all, cross_all)
     return (panel_rows, solved_cross)

time: 511 us -> 529 us (1.035)
  waiting for transfers between devices: 212 us -> 265 us
  blocking collectives: 211 us -> 169 us
  starting transfers between devices: 0.15 us -> 7.98 us
    reduce_scatter x1, waiting for transfers between devices: 0.02 us -> 103 us  [body(): lax.psum_scatter(gram_part, 'tok', scatter_dimension=0, tiled=True)]
    all_gather x1 -> x0, blocking collectives: 52.8 us -> none  [body(): lax.all_gather(cross_rows, 'tok', axis=0, tiled=True)]
    reduce_scatter x1, waiting for transfers between devices: 116 us -> 90.3 us  [body(): lax.psum_scatter(cross_part, 'tok', scatter_dimension=0, tiled=True)]
    all_gather x1, waiting for transfers between devices: 24.7 us -> 0.02 us  [body(): lax.all_gather(proj, 'tok', axis=0, tiled=True)]
    all_gather x1, blocking collectives: 36.4 us -> 58.4 us  [body(): diag_sum = lax.all_gather(summed, 'feat', axis=0, tiled=True)]
    all_gather x1, blocking collectives: 67.7 us -> 52.8 us  [body(): lax.all_gather(gram_rows, 'tok', axis=0, tiled=True)]
    all_to_all x0 -> x1, starting transfers between devices: none -> 7.65 us  [body(): lax.all_to_all(jnp.stack([cross_rows] * lax.axis_size('tok')), 'tok', 0, 0)]
  transfers between devices with their start and end apart: 4 -> 5, of which waited for: 3 -> 3; matrix products, arithmetic and copies ran while one was open for 12% -> 12% of each run, Pallas kernels for 0% -> 0%
where the time goes in v1:
time: 529 us; the launch traced here: 528 us
  waiting for transfers between devices  265 us (50%)
  blocking collectives  169 us (32%)
  other arithmetic  57 us (11%)
  between operations  15.9 us (3%)
  matrix products  8.4 us (2%)
  starting transfers between devices  7.98 us (2%)
  local copies, waits for them, and re-layouts  5.31 us (1%)
    reduce_scatter x1, waiting for transfers between devices, body(): lax.psum_scatter(gram_part, 'tok', scatter_dimension=0, tiled=True)  103 us
    reduce_scatter x1, waiting for transfers between devices, body(): lax.psum_scatter(cross_part, 'tok', scatter_dimension=0, tiled=True)  90.3 us
    all_gather x1, waiting for transfers between devices, body(): token_full = lax.all_gather(tokens, 'feat', axis=1, tiled=True)  69.6 us
    all_gather x1, blocking collectives, body(): diag_sum = lax.all_gather(summed, 'feat', axis=0, tiled=True)  58.4 us
    psum x1, blocking collectives, body(): summed = lax.psum(partial_value, 'tok')  57.5 us
    all_gather x1, blocking collectives, body(): lax.all_gather(gram_rows, 'tok', axis=0, tiled=True)  52.8 us
    another operation x6, other arithmetic, body(): factor = jnp.linalg.cholesky(diag_block)  34 us
    another operation x5, other arithmetic, solve_pair(): lax.linalg.triangular_solve(factor, gram_part, left_side=True, lower=True)  20.4 us
  transfers between devices with their start and end apart: 5, of which 3 were waited for; matrix products, arithmetic and copies ran while one was open for 12% of the time, Pallas kernels for 0%

profile of v1, /device:TPU:6, one launch (start us, length us, event | category | flops | bytes accessed | tf_op | source)
XLA Modules:
  0.0 528.1 jit_solution(9881522464720458874)
XLA Ops:
  7.2 0.0 all-gather.3.cloned.1.call-start
  7.2 0.7 all-gather.3.cloned.1.call-update
  7.9 0.0 all-gather.5.cloned.1.call-start
  7.9 0.7 all-gather.5.cloned.1.call-update
  8.6 0.0 reduce-scatter.5.cloned.1.call-start
  9.4 69.6 %all-gather.3.cloned.1.call-done = bf16[64,8192]{1,0:T(8,128)(2,1)} async-done(((bf16[64,256]{1,0:T(8,128)(2,1)}), bf16[64,8192]{1,0:T(8,128)(2,1)}) %all-gather.3.cloned.1.call-update) | async-done | bytes 1048592 | tf_op jit(solution)/shard_map/all_gather | solution.py:18
  79.0 0.0 copy-start
  79.0 1.1 fusion.30
  80.2 57.5 %psum.7 = f32[8,256]{1,0:T(8,128)S(1)} all-reduce(f32[8,256]{1,0:T(8,128)S(1)} %fusion.30), channel_id=1, replica_groups=mesh['tok'=16,'feat'=32] {'tok'}, use_global_device_ids=true, to_apply=%region_0.0 | all-reduce | flops 2048 | bytes 16384 | tf_op jit(solution)/shard_map/psum | solution.py:51
  137.7 58.4 %all_gather.13 = f32[256,256]{1,0:T(8,128)S(1)} all-gather(f32[8,256]{1,0:T(8,128)S(1)} %psum.7), channel_id=1, replica_groups=mesh['tok'=16,'feat'=32] {'feat'}, dimensions={0}, use_global_device_ids=true | all-gather | bytes 270336 | tf_op jit(solution)/shard_map/all_gather | solution.py:52
  196.0 0.0 copy-start.1
  196.0 0.0 copy-start.2
  196.0 0.1 copy.13
  196.2 0.1 copy.14
  196.3 0.1 fusion.14
  196.4 11.7 %cholesky.49 = f32[128,128]{1,0:T(8,128)S(1)} custom-call(f32[128,128]{1,0:T(8,128)S(1)} %cholesky.115), custom_call_target="Cholesky" | custom-call | tf_op jit(solution)/shard_map/jit(cholesky)/cholesky | solution.py:54
  208.1 0.1 copy.15
  208.3 9.8 %custom-call.14 = f32[1,128,128]{1,2,0:T(8,128)S(1)} custom-call(f32[1,128,128]{2,1,0:T(8,128)S(1)} %get-tuple-element.46), custom_call_target="InvertDiagBlocksLowerTriangular" | custom-call | tf_op jit(solution)/shard_map/jit(cholesky)/cholesky | solution.py:54
  218.1 0.2 fusion.19
  218.3 0.1 copy.16
  218.4 0.0 copy-done
  218.4 0.3 fusion
  218.7 0.0 all-gather.5.cloned.1.call-done
  218.7 0.0 copy-done.1
  218.8 0.0 copy-done.2
  218.8 4.0 fusion.7
  222.8 0.0 reduce-scatter.5.cloned.1.call-update
  222.8 0.2 reduce-scatter.3.cloned.1.call-start
  223.0 0.3 convolution_subtract_fusion.2
  223.3 11.7 %cholesky.103 = f32[128,128]{1,0:T(8,128)S(1)} custom-call(f32[128,128]{1,0:T(8,128)S(1)} %convolution_subtract_fusion.2), custom_call_target="Cholesky" | custom-call | tf_op jit(solution)/shard_map/jit(cholesky)/cholesky | solution.py:54
  235.0 0.1 copy.17
  235.1 0.9 fusion.28
  236.1 0.0 reduce-scatter.3.cloned.1.call-update
  236.1 0.7 compare_reduce_fusion
  238.1 0.1 broadcast.138
  238.1 4.0 while.4
  238.1 0.6 fusion.46
  238.7 1.3 dynamic-slice.9
  240.0 0.1 copy.22
  240.1 0.6 fusion.46
  240.7 1.3 dynamic-slice.9
  242.0 0.1 copy.22
  242.1 19.7 %custom-call.16 = f32[2,128,128]{1,2,0:T(8,128)S(1)} custom-call(f32[2,128,128]{2,1,0:T(8,128)S(1)} %get-tuple-element.17), custom_call_target="InvertDiagBlocksLowerTriangular" | custom-call | tf_op jit(solution)/shard_map/triangular_solve/custom-call.0 | solution.py:12
  261.8 90.3 %reduce-scatter.5.cloned.1.call-done = f32[16,256]{1,0:T(8,128)} async-done(((f32[256,256]{1,0:T(8,128)}), f32[16,256]{1,0:T(8,128)}) %reduce-scatter.5.cloned.1.call-update) | async-done | bytes 16400 | tf_op jit(solution)/shard_map/reduce_scatter | solution.py:35
  352.1 0.7 broadcast_multiply_fusion
  352.8 0.7 stack.2
  353.6 7.6 %all-to-all-start = ((f32[16,16,256]{2,1,0:T(8,128)}), f32[16,16,256]{2,1,0:T(8,128)S(1)}, u32[]{:S(2)}, u32[]{:S(2)}) async-start(f32[16,16,256]{2,1,0:T(8,128)} %stack.2), calls=%async_computation.2 | async-start | bytes 524288 | tf_op jit(solution)/shard_map/all_to_all | solution.py:58
  361.2 103.5 %reduce-scatter.3.cloned.1.call-done = f32[16,256]{1,0:T(8,128)} async-done(((f32[256,256]{1,0:T(8,128)}), f32[16,256]{1,0:T(8,128)}) %reduce-scatter.3.cloned.1.call-update) | async-done | bytes 16400 | tf_op jit(solution)/shard_map/reduce_scatter | solution.py:34
  464.7 0.8 select_add_fusion.1
  465.5 52.8 %all_gather.14 = f32[256,256]{1,0:T(8,128)S(1)} all-gather(f32[16,256]{1,0:T(8,128)S(1)} %select_add_fusion.1), channel_id=1, replica_groups=mesh['tok'=16,'feat'=32] {'tok'}, dimensions={0}, use_global_device_ids=true | all-gather | bytes 278528 | tf_op jit(solution)/shard_map/all_gather | solution.py:56
  518.2 0.3 fusion.17
  518.6 0.3 convolution_subtract_fusion.1
  518.9 0.3 fusion.24
  519.2 0.7 pad_maximum_fusion
  519.9 0.0 all-to-all-done
  519.9 0.3 fusion.15
  520.2 0.3 convolution_subtract_fusion
  520.6 0.3 fusion.23
  520.9 0.7 pad_maximum_fusion.1
  (17 shorter events, 0.2 us)
Async XLA Ops:
  7.2 71.9 %all-gather.3.cloned.1.call-start = ((), (), s32[]{:S(2)}) async-start(), calls=%async_computation.3 | async-start | bytes 1081344 | tf_op jit(solution)/shard_map/all_gather | solution.py:18
  7.9 210.8 %all-gather.5.cloned.1.call-start = ((), (), s32[]{:S(2)}) async-start(), calls=%async_computation.5 | async-start | bytes 4456448 | tf_op jit(solution)/shard_map/all_gather | solution.py:24
  8.6 343.5 %reduce-scatter.5.cloned.1.call-start = ((), (), s32[]{:S(2)}) async-start(), calls=%async_computation.6 | async-start | bytes 278528 | tf_op jit(solution)/shard_map/reduce_scatter | solution.py:35
  79.0 139.3 %copy-start = (bf16[64,8192]{1,0:T(8,128)(2,1)S(1)}, bf16[64,8192]{1,0:T(8,128)(2,1)}, u32[]{:S(2)}) copy-start(bf16[64,8192]{1,0:T(8,128)(2,1)} %all-gather.3.cloned.1.call-done) | copy-start | bytes 3145732
  196.0 22.7 %copy-start.1 = (bf16[64,256]{1,0:T(8,128)(2,1)S(1)}, bf16[64,256]{1,0:T(8,128)(2,1)}, u32[]{:S(2)}) copy-start(bf16[64,256]{1,0:T(8,128)(2,1)} %param.6) | copy-start | bytes 98308
  196.0 22.7 %copy-start.2 = (f32[8192]{0:T(1024)S(1)}, f32[8192]{0:T(1024)}, u32[]{:S(2)}) copy-start(f32[8192]{0:T(1024)} %param.7) | copy-start | bytes 98308
  222.8 241.9 %reduce-scatter.3.cloned.1.call-start = ((), (), s32[]{:S(2)}) async-start(), calls=%async_computation.4 | async-start | bytes 278528 | tf_op jit(solution)/shard_map/reduce_scatter | solution.py:34
  353.6 166.4 %all-to-all-start = ((f32[16,16,256]{2,1,0:T(8,128)}), f32[16,16,256]{2,1,0:T(8,128)S(1)}, u32[]{:S(2)}, u32[]{:S(2)}) async-start(f32[16,16,256]{2,1,0:T(8,128)} %stack.2), calls=%async_computation.2 | async-start | bytes 524288 | tf_op jit(solution)/shard_map/all_to_all | solution.py:58
Sparse Core Ops, SparseCore 0:
  10.0 68.9 all-gather.2
  82.1 130.5 all-gather.4
  222.9 129.1 reduce-scatter.4
  356.6 108.0 reduce-scatter.2
